TPU v7x, 32 devices: a whole 2x2x4 slice. The times are simulated.
32 devices in a mesh: groups: 2 (over y), frames: 4 (over z), rows: 2 (over x), heads: 2 (over core).
Axes of the slice: x: 2, y: 2, z: 4, core: 2. Of those that a mesh axis runs over, the one named last changes fastest.
Arguments:
- queries: bfloat16 [8, 16, 64, 2240], P(('groups', 'frames'), 'rows', None, 'heads'), parts along dimension 0, may hold values from -2 to 1
- keys: bfloat16 [8, 16, 64, 2240], P(('groups', 'frames'), 'rows', None, 'heads'), parts along dimension 0, may hold values from -6 to 6
- values: bfloat16 [8, 16, 64, 2240], P(('groups', 'frames'), 'rows', None, 'heads'), parts along dimension 0, may hold values from -20 to 20
- out_weight: bfloat16 [2240, 2240], P('heads', 'frames'), may hold values from -0.125 to 0.125
Outputs:
- projected: bfloat16 [8, 16, 64, 2240], P(('groups', 'frames'), 'rows', None, 'heads'), parts along dimension 0
There are 2 independent parts, one for each index of `groups`. A program takes and returns all parts, laid end to end along the dimension named above; an argument that names none is the same for every part. Nothing has to cross between parts.
All inputs are finite; a program needn't handle non-finite values.
Results may differ from a plain program's by a relative error of at most 0.0049.
Values may be sent and summed in bfloat16 or wider, within the bound.
A program may use at most 64 MiB of HBM per device.

v0:
```python
import jax
import jax.numpy as jnp
from jax import lax
from jax.sharding import PartitionSpec as P

HD = 112


EPS = 1e-06


def prefix_before(local):
    position = lax.axis_index("frames") * local[0].shape[0]
    pieces = (
        lax.all_gather(local[0], "frames", axis=0, tiled=True),
        lax.all_gather(local[1], "frames", axis=0, tiled=True),
    )
    count = pieces[0].shape[0]
    keep = jnp.arange(count, dtype=jnp.int32) < position
    states = jnp.sum(jnp.where(keep[:, None, None, None], pieces[0], 0.0), axis=0, keepdims=True)
    totals = jnp.sum(jnp.where(keep[:, None, None], pieces[1], 0.0), axis=0, keepdims=True)
    return (states, totals)


def shards(queries, keys, values, out_weight):
    frames_here, rows_here, columns, features = queries.shape
    heads_here = features // HD
    shape4 = (frames_here, rows_here * columns, heads_here, HD)
    query_pos = jnp.maximum(queries, 0).reshape(shape4).astype(jnp.float32)
    key_pos = jnp.maximum(keys, 0).reshape(shape4)
    value_rows = values.reshape(shape4)
    frame_state = jnp.einsum(
        "fthd,fthe->fhde", key_pos, value_rows, preferred_element_type=jnp.float32
    )
    frame_norm = jnp.sum(key_pos.astype(jnp.float32), axis=1)
    own = lax.psum((frame_state, frame_norm), "rows")
    earlier = prefix_before(own)
    state = own[0] + earlier[0]
    norm = own[1] + earlier[1]
    numer = jnp.einsum("fthd,fhde->fthe", query_pos, state, precision=lax.Precision.HIGHEST)
    denom = jnp.einsum("fthd,fhd->fth", query_pos, norm, precision=lax.Precision.HIGHEST)
    attended = (numer / (denom[..., None] + EPS)).astype(jnp.bfloat16)
    attended = attended.reshape(frames_here * rows_here * columns, features)
    terms = jnp.dot(
        attended,
        lax.all_gather(out_weight, "frames", axis=1, tiled=True),
        preferred_element_type=jnp.float32,
    )
    mixed = lax.psum_scatter(terms, "heads", scatter_dimension=1, tiled=True).astype(jnp.bfloat16)
    return mixed.reshape(frames_here, rows_here, columns, mixed.shape[1])


def solution(mesh):
    return jax.shard_map(
        shards,
        mesh=mesh,
        in_specs=(
            P(("groups", "frames"), "rows", None, "heads"),
            P(("groups", "frames"), "rows", None, "heads"),
            P(("groups", "frames"), "rows", None, "heads"),
            P("heads", "frames"),
        ),
        out_specs=P(("groups", "frames"), "rows", None, "heads"),
        check_vma=False,
    )
```

profile of v0, /device:TPU:24, one launch (start us, length us, event | category | flops | bytes accessed | tf_op | source)
XLA Modules:
  0.0 226.9 jit_solution(10531918947951689015)
XLA Ops:
  6.5 0.0 all-reduce.2.cloned.1.call-start
  6.5 1.4 broadcast_maximum_fusion.1
  7.9 2.5 %reshape.59 = bf16[512,10,112]{2,1,0:T(8,128)(2,1)S(1)} reshape(bf16[1,8,64,1120]{3,2,1,0:T(8,128)(2,1)S(1)} %broadcast_maximum_fusion.1) | data formatting | bytes 2293760 | tf_op jit(solution)/shard_map/reshape
  10.4 4.9 %reshape.60 = bf16[512,10,112]{2,1,0:T(8,128)(2,1)} reshape(bf16[1,8,64,1120]{3,2,1,0:T(8,128)(2,1)} %param.6) | data formatting | bytes 2293760 | tf_op jit(solution)/shard_map/reshape.1
  15.4 3.5 %fusion.4 = f32[1,10,112,112]{3,2,1,0:T(8,128)} fusion(bf16[512,10,112]{2,1,0:T(8,128)(2,1)} %reshape.60, bf16[512,10,112]{2,1,0:T(8,128)(2,1)S(1)} %reshape.59), kind=kOutput, calls=%fused_computation.7 | convolution fusion | flops 128450560 | bytes 2795520 | tf_op jit(solution)/shard_map/fthd,fthe->fhde/dot_general | solution.py:32
  18.9 0.0 copy-start
  18.9 0.0 all-reduce.2.cloned.1.call-update
  18.9 0.0 all-gather.3.cloned.1.call-start
  19.0 30.8 %all-reduce.2.cloned.1.call-done = f32[1,10,112,112]{3,2,1,0:T(8,128)} async-done(((f32[1,10,112,112]{3,2,1,0:T(8,128)}), f32[1,10,112,112]{3,2,1,0:T(8,128)}) %all-reduce.2.cloned.1.call-update) | async-done | bytes 501776 | tf_op jit(solution)/shard_map/psum | solution.py:36
  49.8 0.0 all-gather.3.cloned.1.call-update
  49.8 0.0 all-gather.5.cloned.1.call-start
  49.8 0.7 all-gather.5.cloned.1.call-update
  50.5 0.0 reduce-scatter.2.cloned.1.call-start
  50.6 0.0 copy-done
  50.6 0.3 convert_reduce_fusion
  50.9 0.1 reduce_sum.31
  50.9 1.4 broadcast_maximum_fusion
  52.3 2.5 %reshape.62 = bf16[512,10,112]{2,1,0:T(8,128)(2,1)S(1)} reshape(bf16[1,8,64,1120]{3,2,1,0:T(8,128)(2,1)S(1)} %broadcast_maximum_fusion) | data formatting | bytes 2293760 | tf_op jit(solution)/shard_map/reshape.4
  54.8 1.6 copy.18
  56.4 5.0 %psum.15 = f32[1,10,112]{2,1,0:T(8,128)S(1)} all-reduce(f32[1,10,112]{2,1,0:T(8,128)S(1)} %reduce_sum.31), channel_id=1, replica_groups=mesh['groups'=2,'frames'=4,'rows'=2,'heads'=2] {'rows'}, use_global_device_ids=true, to_apply=%region_3.4 | all-reduce | flops 1120 | bytes 8960 | tf_op jit(solution)/shard_map/psum | solution.py:36
  61.4 13.8 %all_gather.10 = f32[4,10,112]{2,1,0:T(8,128)S(1)} all-gather(f32[1,10,112]{2,1,0:T(8,128)S(1)} %psum.15), channel_id=1, replica_groups=mesh['groups'=2,'frames'=4,'rows'=2,'heads'=2] {'frames'}, dimensions={0}, use_global_device_ids=true | all-gather | bytes 22400 | tf_op jit(solution)/shard_map/all_gather | solution.py:16
  75.3 0.1 select_reduce_fusion.1
  75.3 0.6 fusion.12
  75.9 0.0 copy-start.1
  75.9 22.7 %all-gather.3.cloned.1.call-done = f32[4,10,112,112]{3,2,1,0:T(8,128)} async-done(((f32[1,10,112,112]{3,2,1,0:T(8,128)}), f32[4,10,112,112]{3,2,1,0:T(8,128)}) %all-gather.3.cloned.1.call-update) | async-done | bytes 2007056 | tf_op jit(solution)/shard_map/all_gather | solution.py:15
  98.7 2.0 select_reduce_fusion
  100.7 0.0 copy-done.1
  100.7 2.1 fusion
  102.8 92.1 %all-gather.5.cloned.1.call-done = bf16[1120,2240]{0,1:T(8,128)(2,1)} async-done(((bf16[1120,560]{0,1:T(8,128)(2,1)}), bf16[1120,2240]{0,1:T(8,128)(2,1)}) %all-gather.5.cloned.1.call-update) | async-done | bytes 5017616 | tf_op jit(solution)/shard_map/all_gather | solution.py:46
  194.9 8.1 %fusion.14 = f32[512,2240]{0,1:T(8,128)} fusion(bf16[1120,2240]{0,1:T(8,128)(2,1)} %all-gather.5.cloned.1.call-done, bf16[512,1120]{0,1:T(8,128)(2,1)} %bitcast.45), kind=kOutput, calls=%fused_computation.20 | convolution fusion | flops 2569011200 | bytes 10752000 | tf_op jit(solution)/shard_map/dot_general | solution.py:44
  203.0 0.0 reduce-scatter.2.cloned.1.call-update
  203.0 14.2 %reduce-scatter.2.cloned.1.call-done = f32[512,1120]{0,1:T(8,128)} async-done(((f32[512,2240]{0,1:T(8,128)}), f32[512,1120]{0,1:T(8,128)}) %reduce-scatter.2.cloned.1.call-update) | async-done | bytes 2293776 | tf_op jit(solution)/shard_map/reduce_scatter | solution.py:49
  217.2 1.8 convert_element_type.15
  219.0 1.4 copy.19
  (3 shorter events, 0.0 us)
Async XLA Ops:
  6.5 43.2 %all-reduce.2.cloned.1.call-start = ((), (), s32[]{:S(2)}) async-start(), calls=%async_computation.1 | async-start | bytes 1146880 | tf_op jit(solution)/shard_map/psum | solution.py:36
  18.9 31.7 %copy-start = (bf16[1,8,64,1120]{3,2,1,0:T(8,128)(2,1)S(1)}, bf16[1,8,64,1120]{3,2,1,0:T(8,128)(2,1)}, u32[]{:S(2)}) copy-start(bf16[1,8,64,1120]{3,2,1,0:T(8,128)(2,1)} %param.5) | copy-start | bytes 3440644
  18.9 79.7 %all-gather.3.cloned.1.call-start = ((), (), s32[]{:S(2)}) async-start(), calls=%async_computation.2 | async-start | bytes 2867200 | tf_op jit(solution)/shard_map/all_gather | solution.py:15
  49.8 145.1 %all-gather.5.cloned.1.call-start = ((), (), s32[]{:S(2)}) async-start(), calls=%async_computation.3 | async-start | bytes 6451200 | tf_op jit(solution)/shard_map/all_gather | solution.py:46
  50.5 166.7 %reduce-scatter.2.cloned.1.call-start = ((), (), s32[]{:S(2)}) async-start(), calls=%async_computation.4 | async-start | bytes 6881280 | tf_op jit(solution)/shard_map/reduce_scatter | solution.py:49
  75.9 24.8 %copy-start.1 = (f32[1,10,112,112]{3,2,1,0:T(8,128)S(1)}, f32[1,10,112,112]{3,2,1,0:T(8,128)}, u32[]{:S(2)}) copy-start(f32[1,10,112,112]{3,2,1,0:T(8,128)} %all-reduce.2.cloned.1.call-done) | copy-start | bytes 1505284
Sparse Core Ops, SparseCore 0:
  19.0 30.6 all-reduce.1
  51.3 47.2 all-gather.2
  100.2 94.6 all-gather.4
  203.2 13.9 reduce-scatter.1
where the time goes:
time: 229 us; the launch traced here: 227 us
  waiting for transfers between devices  161 us (70%)
  blocking collectives  18.8 us (8%)
  matrix products  14.3 us (6%)
  between operations  13.2 us (6%)
  local copies, waits for them, and re-layouts  13 us (6%)
  other arithmetic  6.91 us (3%)
    all_gather x1, waiting for transfers between devices, shards(): lax.all_gather(out_weight, 'frames', axis=1, tiled=True)  92.1 us
    psum x1, waiting for transfers between devices, shards(): own = lax.psum((frame_state, frame_norm), 'rows')  30.8 us
    all_gather x1, waiting for transfers between devices, prefix_before(): lax.all_gather(local[0], 'frames', axis=0, tiled=True)  22.7 us
    reduce_scatter x1, waiting for transfers between devices, shards(): lax.psum_scatter(terms, 'heads', scatter_dimension=1, tiled=True)  14.2 us
    all_gather x1, blocking collectives, prefix_before(): lax.all_gather(local[1], 'frames', axis=0, tiled=True)  13.8 us
    another operation x3, local copies, waits for them, and re-layouts  9.01 us
    dot_general x1, matrix products, shards(): jnp.dot(attended, lax.all_gather(out_weight, 'frames', axis=1, tiled=True...  8.06 us
    psum x1, blocking collectives, shards(): own = lax.psum((frame_state, frame_norm), 'rows')  5 us
  transfers between devices with their start and end apart: 4, of which 4 were waited for; matrix products, arithmetic and copies ran while one was open for 5% of the time, Pallas kernels for 0%

commit v1 on v0

--- a/solution.py
+++ b/solution.py
@@ -1,12 +1,16 @@
+import functools
+
 import jax
 import jax.numpy as jnp
 from jax import lax
+from jax.experimental import pallas as pl
+from jax.experimental.pallas import tpu as pltpu
 from jax.sharding import PartitionSpec as P
 
 HD = 112
-
-
 EPS = 1e-06
+LANES = 128
+MESH = pl.DeviceIdType.MESH
 
 
 def prefix_before(local):
@@ -22,7 +26,7 @@
     return (states, totals)
 
 
-def shards(queries, keys, values, out_weight):
+def general(queries, keys, values, out_weight):
     frames_here, rows_here, columns, features = queries.shape
     heads_here = features // HD
     shape4 = (frames_here, rows_here * columns, heads_here, HD)
@@ -50,9 +54,353 @@
     return mixed.reshape(frames_here, rows_here, columns, mixed.shape[1])
 
 
+A, D, X, Y = 0, 1, 2, 3
+
+
+def kernel(
+    nz, q_ref, k_ref, v_ref, w_ref, out_ref,
+    wbuf, att, st, own5, rs_send, rs_recv, z_send, z_recv, fin,
+    w_recv, own_send, rel_send, block_sem, rs_sem, zs_send, zs_recv, ag_sem, at_send, at_recv,
+):
+    y, z = lax.axis_index("groups"), lax.axis_index("frames")
+    x, c = lax.axis_index("rows"), lax.axis_index("heads")
+    heads, _, wide = w_ref.shape
+    tokens = q_ref.shape[0]
+    half = heads // 2
+    slots = nz // 2
+    via_x = half * 2 // 5
+    home = z // slots
+
+    def dev(x_=None, y_=None, z_=None, c_=None):
+        return (
+            y if y_ is None else y_,
+            z if z_ is None else z_,
+            x if x_ is None else x_,
+            c if c_ is None else c_,
+        )
+
+    x_nb, y_nb, partner = dev(x_=1 - x), dev(y_=1 - y), dev(c_=1 - c)
+
+    barrier = pltpu.get_barrier_semaphore()
+    greeted = [x_nb, y_nb, partner]
+    for step in range(1, nz):
+        for core in range(2):
+            greeted.append(dev(z_=lax.rem(z + step, nz), c_=core))
+    for device in greeted:
+        pl.semaphore_signal(barrier, inc=1, device_id=device, device_id_type=MESH)
+    pl.semaphore_wait(barrier, len(greeted))
+
+    def remote(src, dst, send, recv, device):
+        return pltpu.make_async_remote_copy(
+            src_ref=src, dst_ref=dst, send_sem=send, recv_sem=recv,
+            device_id=device, device_id_type=MESH,
+        )
+
+    mine = lax.rem(x + y + c, 2)
+    kind = jnp.where(c == x, A, D)
+
+    def own_copy(side, j):
+        target = z + 1 - 2 * side
+        head = mine * half + j
+        return remote(
+            w_ref.at[head],
+            wbuf.at[lax.rem(z, slots), c * heads + head, pl.ds(0, HD)],
+            own_send.at[side, j],
+            w_recv.at[lax.rem(z, slots), kind, j],
+            dev(z_=target, c_=home),
+        )
+
+    def own_each(act):
+        for side in range(2):
+            @pl.when((z < nz - 1) if side == 0 else (z > 0))
+            def _():
+                def body(j, carry):
+                    act(own_copy(side, j))
+                    return carry
+                lax.fori_loop(0, half, body, 0)
+
+    @pl.when(c == x)
+    def _():
+        own_each(lambda copy: copy.start())
+
+    block_dst = wbuf.at[lax.rem(z, slots), pl.ds(c * heads, heads), pl.ds(0, HD)]
+    block_local = pltpu.make_async_copy(w_ref, block_dst, block_sem.at[0])
+    block_out = remote(w_ref, block_dst, block_sem.at[1], block_sem.at[2], partner)
+
+    @pl.when(home == c)
+    def _():
+        block_local.start()
+
+    @pl.when(home != c)
+    def _():
+        block_out.start()
+
+    wbuf[:, :, HD:, :] = jnp.zeros((slots, 2 * heads, LANES - HD, wide), wbuf.dtype)
+
+    base = {
+        A: x * heads + y * half,
+        D: (1 - x) * heads + (1 - y) * half,
+        X: (1 - x) * heads + y * half,
+        Y: x * heads + (1 - y) * half,
+    }
+
+    def slot(i):
+        s = jnp.where(z <= slots * c, i, slots - 1 - i)
+        source = slots * c + s
+        return s, source, jnp.abs(source - z)
+
+    def relay(s, what, j, lane, to_kind, device):
+        ref = wbuf.at[s, base[what] + j, pl.ds(0, HD)]
+        return remote(ref, ref, rel_send.at[s, lane, j], w_recv.at[s, to_kind, j], device)
+
+    def arrived(s, what, j):
+        ref = wbuf.at[s, base[what] + j, pl.ds(0, HD)]
+        remote(ref, ref, rel_send.at[s, 0, j], w_recv.at[s, what, j], x_nb).wait_recv()
+
+    def relays_a(s, source, j):
+        onward = jnp.where(source < z, z + 1, z - 1)
+        target = jnp.clip(onward, 0, nz - 1)
+        return (
+            ((onward >= 0) & (onward < nz), relay(s, A, j, 2, A, dev(z_=target))),
+            (None, relay(s, A, j, 0, X, x_nb)),
+            (None, relay(s, A, j, 1, Y, y_nb)),
+        )
+
+    def on_a(i, wanted):
+        s, source, far = slot(i)
+
+        @pl.when(wanted(far))
+        def _():
+            def body(j, carry):
+                arrived(s, A, j)
+                for needed, copy in relays_a(s, source, j):
+                    if needed is None:
+                        copy.start()
+                    else:
+                        @pl.when(needed)
+                        def _():
+                            copy.start()
+                return carry
+            lax.fori_loop(0, half, body, 0)
+
+    def on_xy(i):
+        s, source, far = slot(i)
+
+        @pl.when(far > 0)
+        def _():
+            def first(j, carry):
+                arrived(s, X, j)
+                arrived(s, Y, j)
+
+                @pl.when(far > 1)
+                def _():
+                    relay(s, Y, j, 3, D, x_nb).start()
+                return carry
+
+            def second(j, carry):
+                arrived(s, X, j)
+                arrived(s, Y, j)
+
+                @pl.when(far > 1)
+                def _():
+                    relay(s, X, j, 3, D, y_nb).start()
+                return carry
+            lax.fori_loop(0, via_x, first, 0)
+            lax.fori_loop(via_x, half, second, 0)
+
+    def on_d(i):
+        s, source, far = slot(i)
+
+        @pl.when(far > 0)
+        def _():
+            def body(j, carry):
+                arrived(s, D, j)
+                return carry
+            lax.fori_loop(0, half, body, 0)
+
+        @pl.when(far == 0)
+        def _():
+            block_local.wait()
+            other = wbuf.at[lax.rem(z, slots), pl.ds((1 - c) * heads, heads), pl.ds(0, HD)]
+            remote(w_ref, other, block_sem.at[1], block_sem.at[2], partner).wait_recv()
+
+    def drain(i):
+        s, source, far = slot(i)
+
+        @pl.when(far > 0)
+        def _():
+            def body(j, carry):
+                for needed, copy in relays_a(s, source, j):
+                    if needed is None:
+                        copy.wait_send()
+                    else:
+                        @pl.when(needed)
+                        def _():
+                            copy.wait_send()
+
+                @pl.when(far > 1)
+                def _():
+                    relay(s, X, j, 3, D, y_nb).wait_send()
+                return carry
+            lax.fori_loop(0, half, body, 0)
+
+    ones = jnp.ones((tokens, LANES), jnp.bfloat16)
+    for h in range(heads):
+        cols = slice(h * HD, (h + 1) * HD)
+        kp = jnp.maximum(k_ref[:, cols], 0)
+        dims = (((0,), (0,)), ((), ()))
+        st[h, :, :HD] = lax.dot_general(
+            kp, v_ref[:, cols], dims, preferred_element_type=jnp.float32)
+        total = lax.dot_general(kp, ones, dims, preferred_element_type=jnp.float32)
+        st[h, :, HD:] = total[:, HD:]
+
+    rs_send[...] = st[pl.ds((1 - x) * half, half)].astype(jnp.bfloat16)
+    rs = remote(rs_send, rs_recv, rs_sem.at[0], rs_sem.at[1], x_nb)
+    rs.start()
+    for i in range(slots):
+        on_a(i, lambda far: far == 1)
+    rs.wait_recv()
+    own5[...] = st[pl.ds(x * half, half)] + rs_recv[...].astype(jnp.float32)
+    z_send[...] = own5[...].astype(jnp.bfloat16)
+
+    def state_copy(step):
+        target = jnp.minimum(z + step, nz - 1)
+        return remote(z_send, z_recv.at[step - 1], zs_send.at[step - 1], zs_recv.at[step - 1],
+                      dev(z_=target))
+
+    for step in range(1, nz):
+        @pl.when(z + step < nz)
+        def _():
+            state_copy(step).start()
+
+    @pl.when(c != x)
+    def _():
+        own_each(lambda copy: copy.start())
+
+    on_a(0, lambda far: far > 1)
+    for step in range(1, nz):
+        @pl.when(z >= step)
+        def _():
+            state_copy(step).wait_recv()
+            own5[...] += z_recv[step - 1].astype(jnp.float32)
+
+    fin[pl.ds(x * half, half)] = own5[...].astype(jnp.bfloat16)
+    ag = remote(fin.at[pl.ds(x * half, half)], fin.at[pl.ds(x * half, half)],
+                ag_sem.at[0], ag_sem.at[1], x_nb)
+    ag.start()
+    on_xy(0)
+    for i in range(1, slots):
+        on_a(i, lambda far: far > 1)
+    other5 = fin.at[pl.ds((1 - x) * half, half)]
+    remote(other5, other5, ag_sem.at[0], ag_sem.at[1], x_nb).wait_recv()
+
+    lane = lax.broadcasted_iota(jnp.int32, (tokens, LANES), 1)
+
+    def att_copy(h):
+        ref = att.at[c, :, pl.ds(h * LANES, LANES)]
+        return remote(ref, ref, at_send.at[h], at_recv.at[h], partner)
+
+    for h in range(heads):
+        qp = jnp.maximum(q_ref[:, h * HD:(h + 1) * HD], 0)
+        both = jnp.dot(qp, fin[h], preferred_element_type=jnp.float32)
+        share = jnp.where(lane < HD, both / (both[:, HD:HD + 1] + EPS), 0.0)
+        att[c, :, h * LANES:(h + 1) * LANES] = share.astype(jnp.bfloat16)
+        att_copy(h).start()
+    for h in range(heads):
+        ref = att.at[1 - c, :, pl.ds(h * LANES, LANES)]
+        remote(ref, ref, at_send.at[h], at_recv.at[h], partner).wait_recv()
+
+    for i in range(slots):
+        s = slot(i)[0]
+        if i:
+            on_xy(i)
+        on_d(i)
+        out = None
+        for r in range(2):
+            part = jnp.dot(
+                att[r],
+                wbuf[s, r * heads:(r + 1) * heads].reshape(heads * LANES, wide),
+                preferred_element_type=jnp.float32,
+            )
+            out = part if out is None else out + part
+        out = out.astype(out_ref.dtype)
+        for place in range(slots):
+            @pl.when(s == place)
+            def _():
+                out_ref[:, place * wide:(place + 1) * wide] = out
+
+    own_each(lambda copy: copy.wait_send())
+
+    @pl.when(home != c)
+    def _():
+        block_out.wait_send()
+    rs.wait_send()
+    for step in range(1, nz):
+        @pl.when(z + step < nz)
+        def _():
+            state_copy(step).wait_send()
+    ag.wait_send()
+    for h in range(heads):
+        att_copy(h).wait_send()
+    for i in range(slots):
+        drain(i)
+
+
+def fused(nz, queries, keys, values, out_weight):
+    frames_here, rows_here, columns, features = queries.shape
+    tokens = frames_here * rows_here * columns
+    heads, half, wide = features // HD, features // HD // 2, out_weight.shape[1]
+    slots = nz // 2
+    state = (half, HD, LANES)
+    vmem = pl.BlockSpec(memory_space=pltpu.VMEM)
+    bf16, f32 = jnp.bfloat16, jnp.float32
+    dma = pltpu.SemaphoreType.DMA
+    out = pl.pallas_call(
+        functools.partial(kernel, nz),
+        out_shape=jax.ShapeDtypeStruct((tokens, slots * wide), bf16),
+        in_specs=[vmem, vmem, vmem, pl.BlockSpec(memory_space=pl.ANY)],
+        out_specs=vmem,
+        scratch_shapes=[
+            pltpu.VMEM((slots, 2 * heads, LANES, wide), bf16),
+            pltpu.VMEM((2, tokens, heads * LANES), bf16),
+            pltpu.VMEM((heads, HD, LANES), f32),
+            pltpu.VMEM(state, f32),
+            pltpu.VMEM(state, bf16),
+            pltpu.VMEM(state, bf16),
+            pltpu.VMEM(state, bf16),
+            pltpu.VMEM((nz - 1,) + state, bf16),
+            pltpu.VMEM((heads, HD, LANES), bf16),
+            dma((slots, 4, half)),
+            dma((2, half)),
+            dma((slots, 4, half)),
+            dma((3,)),
+            dma((2,)),
+            dma((nz - 1,)),
+            dma((nz - 1,)),
+            dma((2,)),
+            dma((heads,)),
+            dma((heads,)),
+        ],
+        compiler_params=pltpu.CompilerParams(
+            collective_id=0, has_side_effects=True, vmem_limit_bytes=56 * 2**20),
+        name="attend_project",
+    )(
+        queries.reshape(tokens, features),
+        keys.reshape(tokens, features),
+        values.reshape(tokens, features),
+        out_weight.reshape(heads, HD, wide),
+    )
+    return out.reshape(frames_here, rows_here, columns, slots * wide)
+
+
 def solution(mesh):
+    size = dict(mesh.shape)
+    pairs = size["rows"] == 2 and size["groups"] == 2 and size["heads"] == 2
+    body = general
+    if pairs and size["frames"] == 4:
+        body = functools.partial(fused, size["frames"])
     return jax.shard_map(
-        shards,
+        body,
         mesh=mesh,
         in_specs=(
             P(("groups", "frames"), "rows", None, "heads"),

time: 229 us -> 71.3 us (0.31)
  waiting for transfers between devices: 161 us -> 0 us
  Pallas kernels: 0 us -> 66.2 us
  blocking collectives: 18.8 us -> 0 us
  matrix products: 14.3 us -> 0 us
  between operations: 13.2 us -> 0.01 us
  local copies, waits for them, and re-layouts: 13 us -> 4.94 us
  other arithmetic: 6.91 us -> 0 us
    all_gather x2 -> x0, waiting for transfers between devices: 115 us -> none  [the longest x1 92.1 us: shards(): lax.all_gather(out_weight, 'frames', axis=1, tiled=True)]
    pallas_call x0 -> x1, Pallas kernels: none -> 66.2 us  [fused(): pl.pallas_call(functools.partial(kernel, nz), out_shape=jax.ShapeDtypeStr...]
    psum x1 -> x0, waiting for transfers between devices: 30.8 us -> none  [shards(): own = lax.psum((frame_state, frame_norm), 'rows')]
    dot_general x4 -> x0, matrix products: 14.3 us -> none  [the longest x1 8.06 us: shards(): jnp.dot(attended, lax.all_gather(out_weight, 'frames', axis=1, tiled=True...]
    reduce_scatter x1 -> x0, waiting for transfers between devices: 14.2 us -> none  [shards(): lax.psum_scatter(terms, 'heads', scatter_dimension=1, tiled=True)]
    all_gather x1 -> x0, blocking collectives: 13.8 us -> none  [prefix_before(): lax.all_gather(local[1], 'frames', axis=0, tiled=True)]
    another operation x3 -> x0, local copies, waits for them, and re-layouts: 9.01 us -> none
    psum x1 -> x0, blocking collectives: 5 us -> none  [shards(): own = lax.psum((frame_state, frame_norm), 'rows')]
  transfers between devices with their start and end apart: 4 -> 0, of which waited for: 4 -> 0; matrix products, arithmetic and copies ran while one was open for 5% -> 0% of each run, Pallas kernels for 0% -> 0%
where the time goes in v1:
time: 71.3 us; the launch traced here: 71.1 us
  Pallas kernels  66.2 us (93%)
  local copies, waits for them, and re-layouts  4.94 us (7%)
    pallas_call x1, Pallas kernels, fused(): pl.pallas_call(functools.partial(kernel, nz), out_shape=jax.ShapeDtypeStr...  66.2 us
    unnamed x2, local copies, waits for them, and re-layouts  4.94 us

profile of v1, /device:TPU:24, one launch (start us, length us, event | category | flops | bytes accessed | tf_op | source)
XLA Modules:
  0.0 71.1 jit_solution(17418689271400522697)
XLA Ops:
  0.0 2.6 %copy.5 = bf16[1120,560]{1,0:T(8,128)(2,1)} copy(bf16[1120,560]{0,1:T(8,128)(2,1)} %param.7) | data formatting | bytes 2508800 | tf_op args[3]
  2.6 66.2 %attend_project.1 = bf16[512,1120]{1,0:T(8,128)(2,1)} custom-call(bf16[512,1120]{1,0:T(8,128)(2,1)} %bitcast.7, bf16[512,1120]{1,0:T(8,128)(2,1)} %bitcast.8, bf16[512,1120]{1,0:T(8,128)(2,1)} %bitcast.9, bf16[10,112,560]{2,1,0:T(8,128)(2,1)} %bitcast.5), custom_call_target="tpu_custom_call" | custom-call | tf_op jit(solution)/shard_map/attend_project/pallas_call | solution.py:358
  68.7 2.4 %copy.7 = bf16[1,8,64,1120]{3,2,1,0:T(8,128)(2,1)} copy(bf16[1,8,64,1120]{3,2,1,0:T(8,128)(2,1)} %bitcast.6) | data formatting | bytes 2293760

commit v2 on v0

--- a/solution.py
+++ b/solution.py
@@ -1,12 +1,16 @@
+import functools
+
 import jax
 import jax.numpy as jnp
 from jax import lax
+from jax.experimental import pallas as pl
+from jax.experimental.pallas import tpu as pltpu
 from jax.sharding import PartitionSpec as P
 
 HD = 112
-
-
 EPS = 1e-06
+LANES = 128
+MESH = pl.DeviceIdType.MESH
 
 
 def prefix_before(local):
@@ -22,7 +26,7 @@
     return (states, totals)
 
 
-def shards(queries, keys, values, out_weight):
+def general(queries, keys, values, out_weight):
     frames_here, rows_here, columns, features = queries.shape
     heads_here = features // HD
     shape4 = (frames_here, rows_here * columns, heads_here, HD)
@@ -50,9 +54,372 @@
     return mixed.reshape(frames_here, rows_here, columns, mixed.shape[1])
 
 
+A, D, X, Y = 0, 1, 2, 3
+PIECES = 5
+
+
+def kernel(
+    nz, q_hbm, k_hbm, v_hbm, w_ref, out_ref,
+    q_ref, k_ref, v_ref, wbuf, att, st, own5, rs_send, rs_recv, z_recv, fin,
+    in_sem, w_recv, own_send, rel_send, block_sem, rs_out, rs_in, z_out, z_in, ag_out, ag_in, at_sem,
+):
+    y, z = lax.axis_index("groups"), lax.axis_index("frames")
+    x, c = lax.axis_index("rows"), lax.axis_index("heads")
+    chunks = w_ref.shape[0]
+    tokens, features = q_ref.shape
+    wide = w_ref.shape[0] * w_ref.shape[1]
+    heads = features // HD
+    half = heads // 2
+    parts = chunks // 2
+    slots = nz // 2
+    home = z // slots
+    spot = lax.rem(z, slots)
+
+    def dev(x_=None, y_=None, z_=None, c_=None):
+        return (
+            y if y_ is None else y_,
+            z if z_ is None else z_,
+            x if x_ is None else x_,
+            c if c_ is None else c_,
+        )
+
+    x_nb, y_nb, partner = dev(x_=1 - x), dev(y_=1 - y), dev(c_=1 - c)
+
+    loads = [
+        pltpu.make_async_copy(src, dst, in_sem.at[n])
+        for n, (src, dst) in enumerate(((k_hbm, k_ref), (v_hbm, v_ref), (q_hbm, q_ref)))
+    ]
+    for load in loads:
+        load.start()
+
+    barrier = pltpu.get_barrier_semaphore()
+    greeted = [x_nb, y_nb, partner]
+    for step in range(1, nz):
+        for core in range(2):
+            greeted.append(dev(z_=lax.rem(z + step, nz), c_=core))
+    for device in greeted:
+        pl.semaphore_signal(barrier, inc=1, device_id=device, device_id_type=MESH)
+    pl.semaphore_wait(barrier, len(greeted))
+
+    def remote(src, dst, send, recv, device):
+        return pltpu.make_async_remote_copy(
+            src_ref=src, dst_ref=dst, send_sem=send, recv_sem=recv,
+            device_id=device, device_id_type=MESH,
+        )
+
+    def each(count, act, begin=0):
+        def body(j, carry):
+            act(j)
+            return carry
+        lax.fori_loop(begin, count, body, 0)
+
+    mine = lax.rem(x + y + c, 2)
+    kind = jnp.where(c == x, A, D)
+
+    def own_copy(side, j):
+        chunk = mine * parts + j
+        return remote(
+            w_ref.at[chunk],
+            wbuf.at[spot, c, chunk],
+            own_send.at[side, j],
+            w_recv.at[spot, kind, j],
+            dev(z_=z + 1 - 2 * side, c_=home),
+        )
+
+    def own_each(act):
+        for side in range(2):
+            @pl.when((z < nz - 1) if side == 0 else (z > 0))
+            def _():
+                each(parts, lambda j: act(own_copy(side, j)))
+
+    @pl.when(c == x)
+    def _():
+        own_each(lambda copy: copy.start())
+
+    block_local = pltpu.make_async_copy(w_ref, wbuf.at[spot, c], block_sem.at[0])
+    block_out = remote(w_ref, wbuf.at[spot, c], block_sem.at[1], block_sem.at[2], partner)
+
+    @pl.when(home == c)
+    def _():
+        block_local.start()
+
+    @pl.when(home != c)
+    def _():
+        block_out.start()
+
+    base = {A: (x, y * parts), D: (1 - x, (1 - y) * parts),
+            X: (1 - x, y * parts), Y: (x, (1 - y) * parts)}
+
+    def slot(i):
+        s = jnp.where(z <= slots * c, i, slots - 1 - i)
+        source = slots * c + s
+        return s, source, jnp.abs(source - z)
+
+    def relay(s, what, j, lane, to_kind, device):
+        rows, first = base[what]
+        ref = wbuf.at[s, rows, first + j]
+        return remote(ref, ref, rel_send.at[s, lane, j], w_recv.at[s, to_kind, j], device)
+
+    def arrived(s, what, j):
+        relay(s, what, j, 0, what, x_nb).wait_recv()
+
+    def relays_a(s, source, j):
+        onward = jnp.where(source < z, z + 1, z - 1)
+        return (
+            ((onward >= 0) & (onward < nz),
+             relay(s, A, j, 2, A, dev(z_=jnp.clip(onward, 0, nz - 1)))),
+            (None, relay(s, A, j, 0, X, x_nb)),
+            (None, relay(s, A, j, 1, Y, y_nb)),
+        )
+
+    def on_a(i, wanted, j):
+        s, source, far = slot(i)
+
+        @pl.when(wanted(far))
+        def _():
+            arrived(s, A, j)
+            for needed, copy in relays_a(s, source, j):
+                if needed is None:
+                    copy.start()
+                else:
+                    @pl.when(needed)
+                    def _():
+                        copy.start()
+
+    def by_x(far):
+        return jnp.where(far == 2, (2 * parts) // PIECES, parts // PIECES)
+
+    def on_xy(i, wanted, j):
+        s, source, far = slot(i)
+
+        @pl.when(wanted(far))
+        def _():
+            arrived(s, X, j)
+            arrived(s, Y, j)
+
+            @pl.when((far > 1) & (j < by_x(far)))
+            def _():
+                relay(s, Y, j, 3, D, x_nb).start()
+
+            @pl.when((far > 1) & (j >= by_x(far)))
+            def _():
+                relay(s, X, j, 3, D, y_nb).start()
+
+    def on_d(i):
+        s, source, far = slot(i)
+
+        @pl.when(far > 0)
+        def _():
+            each(parts, lambda j: arrived(s, D, j))
+
+        @pl.when(far == 0)
+        def _():
+            block_local.wait()
+            other = wbuf.at[spot, 1 - c]
+            remote(w_ref, other, block_sem.at[1], block_sem.at[2], partner).wait_recv()
+
+    def drain(i):
+        s, source, far = slot(i)
+
+        def one(j):
+            for needed, copy in relays_a(s, source, j):
+                if needed is None:
+                    copy.wait_send()
+                else:
+                    @pl.when(needed)
+                    def _():
+                        copy.wait_send()
+
+            @pl.when(far > 1)
+            def _():
+                relay(s, X, j, 3, D, y_nb).wait_send()
+
+        @pl.when(far > 0)
+        def _():
+            each(parts, one)
+
+    def rs(j):
+        return remote(rs_send.at[j], rs_recv.at[j], rs_out.at[j], rs_in.at[j], x_nb)
+
+    loads[0].wait()
+    loads[1].wait()
+    ones = jnp.ones((tokens, LANES), jnp.bfloat16)
+    for j in range(half):
+        for h in (j, half + j):
+            cols = slice(h * HD, (h + 1) * HD)
+            kp = jnp.maximum(k_ref[:, cols], 0)
+            dims = (((0,), (0,)), ((), ()))
+            st[h, :, :HD] = lax.dot_general(
+                kp, v_ref[:, cols], dims, preferred_element_type=jnp.float32)
+            total = lax.dot_general(kp, ones, dims, preferred_element_type=jnp.float32)
+            st[h, :, HD:] = total[:, HD:]
+        rs_send[j] = st[(1 - x) * half + j].astype(jnp.bfloat16)
+        rs(j).start()
+
+    def up(j):
+        return remote(fin.at[x * half + j], z_recv.at[j], z_out.at[j], z_in.at[j],
+                      dev(z_=jnp.minimum(z + 1, nz - 1)))
+
+    def across(j):
+        ref = fin.at[x * half + j]
+        return remote(ref, ref, ag_out.at[j], ag_in.at[j], x_nb)
+
+    def finish(j, total):
+        fin[x * half + j] = total.astype(jnp.bfloat16)
+
+        @pl.when(z < nz - 1)
+        def _():
+            up(j).start()
+        across(j).start()
+
+    def near_step(j):
+        for i in range(slots):
+            on_a(i, lambda far: far == 1, j)
+        rs(j).wait_recv()
+        total = st[x * half + j] + rs_recv[j].astype(jnp.float32)
+        own5[j] = total
+
+        @pl.when(z == 0)
+        def _():
+            finish(j, total)
+
+    def next_step(j):
+        @pl.when(z > 0)
+        def _():
+            up(j).wait_recv()
+            finish(j, own5[j] + z_recv[j].astype(jnp.float32))
+        for i in range(slots):
+            on_a(i, lambda far: far == 2, j)
+
+    def far_step(j):
+        for i in range(slots):
+            on_a(i, lambda far: far > 2, j)
+        for i in range(slots):
+            on_xy(i, lambda far: far == 2, j)
+
+    each(half, near_step)
+    each(half, next_step)
+
+    @pl.when(c != x)
+    def _():
+        own_each(lambda copy: copy.start())
+
+    each(parts, far_step)
+
+    def across_in(j):
+        ref = fin.at[(1 - x) * half + j]
+        remote(ref, ref, ag_out.at[j], ag_in.at[j], x_nb).wait_recv()
+
+    each(half, across_in)
+
+    loads[2].wait()
+    for h in range(heads):
+        qp = jnp.maximum(q_ref[:, h * HD:(h + 1) * HD], 0)
+        both = jnp.dot(qp, fin[h], preferred_element_type=jnp.float32)
+        share = both[:, :HD] / (both[:, HD:HD + 1] + EPS)
+        att[c, :, h * HD:(h + 1) * HD] = share.astype(jnp.bfloat16)
+    att_out = remote(att.at[c], att.at[c], at_sem.at[0], at_sem.at[1], partner)
+    att_out.start()
+    each(parts, lambda j: [on_xy(i, lambda far: (far == 1) | (far > 2), j) for i in range(slots)] and None)
+    remote(att.at[1 - c], att.at[1 - c], at_sem.at[0], at_sem.at[1], partner).wait_recv()
+
+    for i in range(slots):
+        s = slot(i)[0]
+        on_d(i)
+        out = None
+        for r in range(2):
+            part = lax.dot_general(
+                att[r], wbuf[s, r].reshape(wide, features),
+                (((1,), (1,)), ((), ())), preferred_element_type=jnp.float32,
+            )
+            out = part if out is None else out + part
+        out = out.astype(out_ref.dtype)
+        for place in range(slots):
+            @pl.when(s == place)
+            def _():
+                out_ref[:, place * wide:(place + 1) * wide] = out
+
+    own_each(lambda copy: copy.wait_send())
+
+    @pl.when(home != c)
+    def _():
+        block_out.wait_send()
+
+    def sent(j):
+        rs(j).wait_send()
+        across(j).wait_send()
+
+        @pl.when(z < nz - 1)
+        def _():
+            up(j).wait_send()
+
+    each(half, sent)
+    att_out.wait_send()
+    for i in range(slots):
+        drain(i)
+
+
+def fused(nz, queries, keys, values, out_weight):
+    frames_here, rows_here, columns, features = queries.shape
+    tokens = frames_here * rows_here * columns
+    heads, half, wide = features // HD, features // HD // 2, out_weight.shape[1]
+    slots = nz // 2
+    chunks = 2 * PIECES
+    parts = PIECES
+    width = wide // chunks
+    vmem, hbm = pl.BlockSpec(memory_space=pltpu.VMEM), pl.BlockSpec(memory_space=pl.ANY)
+    bf16, f32 = jnp.bfloat16, jnp.float32
+    dma = pltpu.SemaphoreType.DMA
+    out = pl.pallas_call(
+        functools.partial(kernel, nz),
+        out_shape=jax.ShapeDtypeStruct((tokens, slots * wide), bf16),
+        in_specs=[hbm] * 4,
+        out_specs=vmem,
+        scratch_shapes=[
+            pltpu.VMEM((tokens, features), bf16),
+            pltpu.VMEM((tokens, features), bf16),
+            pltpu.VMEM((tokens, features), bf16),
+            pltpu.VMEM((slots, 2, chunks, width, features), bf16),
+            pltpu.VMEM((2, tokens, features), bf16),
+            pltpu.VMEM((heads, HD, LANES), f32),
+            pltpu.VMEM((half, HD, LANES), f32),
+            pltpu.VMEM((half, HD, LANES), bf16),
+            pltpu.VMEM((half, HD, LANES), bf16),
+            pltpu.VMEM((half, HD, LANES), bf16),
+            pltpu.VMEM((heads, HD, LANES), bf16),
+            dma((3,)),
+            dma((slots, 4, parts)),
+            dma((2, parts)),
+            dma((slots, 4, parts)),
+            dma((3,)),
+            dma((half,)),
+            dma((half,)),
+            dma((half,)),
+            dma((half,)),
+            dma((half,)),
+            dma((half,)),
+            dma((2,)),
+        ],
+        compiler_params=pltpu.CompilerParams(
+            collective_id=0, has_side_effects=True, vmem_limit_bytes=56 * 2**20),
+        name="attend_project",
+    )(
+        queries.reshape(tokens, features),
+        keys.reshape(tokens, features),
+        values.reshape(tokens, features),
+        out_weight.T.reshape(chunks, width, features),
+    )
+    return out.reshape(frames_here, rows_here, columns, slots * wide)
+
+
 def solution(mesh):
+    size = dict(mesh.shape)
+    pairs = size["rows"] == 2 and size["groups"] == 2 and size["heads"] == 2
+    body = general
+    if pairs and size["frames"] == 4:
+        body = functools.partial(fused, size["frames"])
     return jax.shard_map(
-        shards,
+        body,
         mesh=mesh,
         in_specs=(
             P(("groups", "frames"), "rows", None, "heads"),

time: 229 us -> 63.4 us (0.28)
  waiting for transfers between devices: 161 us -> 0 us
  Pallas kernels: 0 us -> 60.9 us
  blocking collectives: 18.8 us -> 0 us
  matrix products: 14.3 us -> 0 us
  between operations: 13.2 us -> 0.01 us
  local copies, waits for them, and re-layouts: 13 us -> 2.37 us
  other arithmetic: 6.91 us -> 0 us
    all_gather x2 -> x0, waiting for transfers between devices: 115 us -> none  [the longest x1 92.1 us: shards(): lax.all_gather(out_weight, 'frames', axis=1, tiled=True)]
    pallas_call x0 -> x1, Pallas kernels: none -> 60.9 us  [fused(): pl.pallas_call(functools.partial(kernel, nz), out_shape=jax.ShapeDtypeStr...]
    psum x1 -> x0, waiting for transfers between devices: 30.8 us -> none  [shards(): own = lax.psum((frame_state, frame_norm), 'rows')]
    dot_general x4 -> x0, matrix products: 14.3 us -> none  [the longest x1 8.06 us: shards(): jnp.dot(attended, lax.all_gather(out_weight, 'frames', axis=1, tiled=True...]
    reduce_scatter x1 -> x0, waiting for transfers between devices: 14.2 us -> none  [shards(): lax.psum_scatter(terms, 'heads', scatter_dimension=1, tiled=True)]
    all_gather x1 -> x0, blocking collectives: 13.8 us -> none  [prefix_before(): lax.all_gather(local[1], 'frames', axis=0, tiled=True)]
    another operation x3 -> x0, local copies, waits for them, and re-layouts: 9.01 us -> none
    psum x1 -> x0, blocking collectives: 5 us -> none  [shards(): own = lax.psum((frame_state, frame_norm), 'rows')]
  transfers between devices with their start and end apart: 4 -> 0, of which waited for: 4 -> 0; matrix products, arithmetic and copies ran while one was open for 5% -> 0% of each run, Pallas kernels for 0% -> 0%
where the time goes in v2:
time: 63.4 us; the launch traced here: 63.2 us
  Pallas kernels  60.9 us (96%)
  local copies, waits for them, and re-layouts  2.37 us (4%)
    pallas_call x1, Pallas kernels, fused(): pl.pallas_call(functools.partial(kernel, nz), out_shape=jax.ShapeDtypeStr...  60.9 us
    unnamed x1, local copies, waits for them, and re-layouts  2.37 us

profile of v2, /device:TPU:24, one launch (start us, length us, event | category | flops | bytes accessed | tf_op | source)
XLA Modules:
  0.0 63.2 jit_solution(8855446844182189129)
XLA Ops:
  0.0 60.9 %attend_project.1 = bf16[512,1120]{1,0:T(8,128)(2,1)} custom-call(bf16[512,1120]{1,0:T(8,128)(2,1)} %bitcast.9, bf16[512,1120]{1,0:T(8,128)(2,1)} %bitcast.10, bf16[512,1120]{1,0:T(8,128)(2,1)} %bitcast.11, bf16[10,56,1120]{2,1,0:T(8,128)(2,1)} %bitcast.8), custom_call_target="tpu_custom_call" | custom-call | tf_op jit(solution)/shard_map/attend_project/pallas_call | solution.py:373
  60.9 2.4 %copy.6 = bf16[1,8,64,1120]{3,2,1,0:T(8,128)(2,1)} copy(bf16[1,8,64,1120]{3,2,1,0:T(8,128)(2,1)} %bitcast.7) | data formatting | bytes 2293760

commit v3 on v2

--- a/solution.py
+++ b/solution.py
@@ -153,7 +153,8 @@
     def slot(i):
         s = jnp.where(z <= slots * c, i, slots - 1 - i)
         source = slots * c + s
-        return s, source, jnp.abs(source - z)
+        ends = (source == 0) | (source == nz - 1)
+        return s, source, jnp.abs(source - z), ends
 
     def relay(s, what, j, lane, to_kind, device):
         rows, first = base[what]
@@ -163,54 +164,65 @@
     def arrived(s, what, j):
         relay(s, what, j, 0, what, x_nb).wait_recv()
 
+    def onward(source):
+        to = jnp.where(source < z, z + 1, z - 1)
+        return (to >= 0) & (to < nz), dev(z_=jnp.clip(to, 0, nz - 1))
+
     def relays_a(s, source, j):
-        onward = jnp.where(source < z, z + 1, z - 1)
+        more, to = onward(source)
         return (
-            ((onward >= 0) & (onward < nz),
-             relay(s, A, j, 2, A, dev(z_=jnp.clip(onward, 0, nz - 1)))),
+            (more, relay(s, A, j, 2, A, to)),
             (None, relay(s, A, j, 0, X, x_nb)),
             (None, relay(s, A, j, 1, Y, y_nb)),
         )
 
-    def on_a(i, wanted, j):
-        s, source, far = slot(i)
-
-        @pl.when(wanted(far))
-        def _():
-            arrived(s, A, j)
-            for needed, copy in relays_a(s, source, j):
-                if needed is None:
-                    copy.start()
-                else:
-                    @pl.when(needed)
-                    def _():
+    def on_a(distance, j):
+        for i in range(slots):
+            s, source, far, ends = slot(i)
+
+            @pl.when(far == distance)
+            def _():
+                arrived(s, A, j)
+                for needed, copy in relays_a(s, source, j):
+                    if needed is None:
                         copy.start()
-
-    def by_x(far):
-        return jnp.where(far == 2, (2 * parts) // PIECES, parts // PIECES)
-
-    def on_xy(i, wanted, j):
-        s, source, far = slot(i)
-
-        @pl.when(wanted(far))
-        def _():
-            arrived(s, X, j)
-            arrived(s, Y, j)
-
-            @pl.when((far > 1) & (j < by_x(far)))
-            def _():
-                relay(s, Y, j, 3, D, x_nb).start()
-
-            @pl.when((far > 1) & (j >= by_x(far)))
-            def _():
-                relay(s, X, j, 3, D, y_nb).start()
-
-    def on_d(i):
-        s, source, far = slot(i)
-
-        @pl.when(far > 0)
-        def _():
-            each(parts, lambda j: arrived(s, D, j))
+                    else:
+                        @pl.when(needed)
+                        def _():
+                            copy.start()
+
+    def on_xy(wanted, j):
+        for i in range(slots):
+            s, source, far, ends = slot(i)
+            by_x = jnp.where(far == 1, (2 * parts) // PIECES, parts // PIECES)
+
+            @pl.when((far > 0) & wanted(far, ends))
+            def _():
+                arrived(s, X, j)
+                arrived(s, Y, j)
+
+                @pl.when(jnp.logical_not(ends) & (j < by_x))
+                def _():
+                    relay(s, Y, j, 3, D, x_nb).start()
+
+                @pl.when(jnp.logical_not(ends) & (j >= by_x))
+                def _():
+                    relay(s, X, j, 3, D, y_nb).start()
+
+    def on_d(i, wanted, j):
+        s, source, far, ends = slot(i)
+
+        @pl.when((far > 0) & wanted(far, ends))
+        def _():
+            arrived(s, D, j)
+            more, to = onward(source)
+
+            @pl.when(ends & more)
+            def _():
+                relay(s, D, j, 3, D, to).start()
+
+    def on_block(i):
+        s, source, far, ends = slot(i)
 
         @pl.when(far == 0)
         def _():
@@ -219,7 +231,8 @@
             remote(w_ref, other, block_sem.at[1], block_sem.at[2], partner).wait_recv()
 
     def drain(i):
-        s, source, far = slot(i)
+        s, source, far, ends = slot(i)
+        more, to = onward(source)
 
         def one(j):
             for needed, copy in relays_a(s, source, j):
@@ -230,7 +243,7 @@
                     def _():
                         copy.wait_send()
 
-            @pl.when(far > 1)
+            @pl.when(jnp.logical_not(ends) | more)
             def _():
                 relay(s, X, j, 3, D, y_nb).wait_send()
 
@@ -255,6 +268,7 @@
             st[h, :, HD:] = total[:, HD:]
         rs_send[j] = st[(1 - x) * half + j].astype(jnp.bfloat16)
         rs(j).start()
+        on_a(1, j)
 
     def up(j):
         return remote(fin.at[x * half + j], z_recv.at[j], z_out.at[j], z_in.at[j],
@@ -272,9 +286,11 @@
             up(j).start()
         across(j).start()
 
+    @pl.when((c != x) & ((z == 0) | (z == nz - 1)))
+    def _():
+        own_each(lambda copy: copy.start())
+
     def near_step(j):
-        for i in range(slots):
-            on_a(i, lambda far: far == 1, j)
         rs(j).wait_recv()
         total = st[x * half + j] + rs_recv[j].astype(jnp.float32)
         own5[j] = total
@@ -284,27 +300,28 @@
             finish(j, total)
 
     def next_step(j):
+        on_a(2, j)
+        on_xy(lambda far, ends: (far == 1) & jnp.logical_not(ends), j)
+
         @pl.when(z > 0)
         def _():
             up(j).wait_recv()
             finish(j, own5[j] + z_recv[j].astype(jnp.float32))
+
+    def far_step(j):
+        on_a(3, j)
         for i in range(slots):
-            on_a(i, lambda far: far == 2, j)
-
-    def far_step(j):
+            on_d(i, lambda far, ends: (far == 1) & ends, j)
+        on_xy(lambda far, ends: (far == 2) & jnp.logical_not(ends), j)
+
+    def last_step(j):
         for i in range(slots):
-            on_a(i, lambda far: far > 2, j)
-        for i in range(slots):
-            on_xy(i, lambda far: far == 2, j)
+            on_d(i, lambda far, ends: (far == 2) & ends, j)
 
     each(half, near_step)
     each(half, next_step)
-
-    @pl.when(c != x)
-    def _():
-        own_each(lambda copy: copy.start())
-
     each(parts, far_step)
+    each(parts, last_step)
 
     def across_in(j):
         ref = fin.at[(1 - x) * half + j]
@@ -320,12 +337,14 @@
         att[c, :, h * HD:(h + 1) * HD] = share.astype(jnp.bfloat16)
     att_out = remote(att.at[c], att.at[c], at_sem.at[0], at_sem.at[1], partner)
     att_out.start()
-    each(parts, lambda j: [on_xy(i, lambda far: (far == 1) | (far > 2), j) for i in range(slots)] and None)
+    each(parts, lambda j: on_xy(lambda far, ends: ends, j))
     remote(att.at[1 - c], att.at[1 - c], at_sem.at[0], at_sem.at[1], partner).wait_recv()
 
     for i in range(slots):
         s = slot(i)[0]
-        on_d(i)
+        on_block(i)
+        each(parts, lambda j: on_d(
+            i, lambda far, ends: (far > 2) | jnp.logical_not(ends), j))
         out = None
         for r in range(2):
             part = lax.dot_general(
@@ -339,7 +358,9 @@
             def _():
                 out_ref[:, place * wide:(place + 1) * wide] = out
 
-    own_each(lambda copy: copy.wait_send())
+    @pl.when((c == x) | (z == 0) | (z == nz - 1))
+    def _():
+        own_each(lambda copy: copy.wait_send())
 
     @pl.when(home != c)
     def _():

time: 63.4 us -> 59.8 us (0.943)
  Pallas kernels: 60.9 us -> 57.2 us
    pallas_call x1, Pallas kernels: 60.9 us -> 57.2 us  [fused(): pl.pallas_call(functools.partial(kernel, nz), out_shape=jax.ShapeDtypeStr...]
where the time goes in v3:
time: 59.8 us; the launch traced here: 59.6 us
  Pallas kernels  57.2 us (96%)
  local copies, waits for them, and re-layouts  2.37 us (4%)
    pallas_call x1, Pallas kernels, fused(): pl.pallas_call(functools.partial(kernel, nz), out_shape=jax.ShapeDtypeStr...  57.2 us
    unnamed x1, local copies, waits for them, and re-layouts  2.37 us

profile of v3, /device:TPU:24, one launch (start us, length us, event | category | flops | bytes accessed | tf_op | source)
XLA Modules:
  0.0 59.6 jit_solution(7791904575720803655)
XLA Ops:
  0.0 57.2 %attend_project.1 = bf16[512,1120]{1,0:T(8,128)(2,1)} custom-call(bf16[512,1120]{1,0:T(8,128)(2,1)} %bitcast.9, bf16[512,1120]{1,0:T(8,128)(2,1)} %bitcast.10, bf16[512,1120]{1,0:T(8,128)(2,1)} %bitcast.11, bf16[10,56,1120]{2,1,0:T(8,128)(2,1)} %bitcast.8), custom_call_target="tpu_custom_call" | custom-call | tf_op jit(solution)/shard_map/attend_project/pallas_call | solution.py:394
  57.3 2.4 %copy.6 = bf16[1,8,64,1120]{3,2,1,0:T(8,128)(2,1)} copy(bf16[1,8,64,1120]{3,2,1,0:T(8,128)(2,1)} %bitcast.7) | data formatting | bytes 2293760
